TPU v7x, 256 devices: a whole 4x4x8 slice. The times are simulated.
256 devices in a mesh: az: 64 (over x, z, core), rg: 4 (over y).
Axes of the slice: x: 4, y: 4, z: 8, core: 2. Of those that a mesh axis runs over, the one named last changes fastest.
Arguments:
- echoes: bfloat16 [2, 2048, 32768], P(None, 'rg', 'az'), may hold values from -6 to 6
- coef_table: bfloat16 [8, 5, 128, 128], replicated, may hold values from -0.3125 to 0.3125
- kern_id: int32 [256], replicated, may hold values from 0 to 7
- band_lo: int32 [256], replicated, may hold values from -2 to 2, as said below
- band_width: int32 [256], replicated, may hold values from 1 to 5
- rate: float32 [2048], P('rg'), may hold values from 4 to 40
Outputs:
- image: bfloat16 [2, 2048, 32768], P(None, ('rg', 'az'))
Inputs may be any that keep to these rules, and one draw needn't show every extreme that they name: band_lo[b] + band_width[b] - 1 <= 2 for every frequency block b.
All inputs are finite; a program needn't handle non-finite values.
Results may differ from a plain program's by a relative error of at most 0.0095.
Values may be sent and summed in bfloat16 or wider, within the bound.
No kernel may reach another device: no remote copies, remote signals or barrier semaphores. Data moves between devices by JAX's collectives and lax.ppermute only.
A program may use at most 64 MiB of HBM per device.

v0:
```python
import math
import jax
import jax.numpy as jnp
from jax import lax
from jax.sharding import PartitionSpec as P

A = 32768
P_SIZE = 512
Q = 64
TILE = 128
FB = 128
FBLK = 256
HT = 2
WMAX = 5
TWO_PI = 2.0 * math.pi


def padded_2(block, sides, width):
    for axis, dim in sides:
        count = lax.axis_size(axis)
        forward = [(i, i + 1) for i in range(count - 1)]
        backward = [(target, source) for source, target in forward]
        low = lax.ppermute(
            lax.slice_in_dim(block, block.shape[dim] - width, None, axis=dim), axis, forward
        )
        high = lax.ppermute(lax.slice_in_dim(block, 0, width, axis=dim), axis, backward)
        block = jnp.concatenate([low, block, high], axis=dim)
    return block


def rotation(first, second, length):
    product = lax.broadcasted_iota(jnp.int32, (first, second), 0) * lax.broadcasted_iota(
        jnp.int32, (first, second), 1
    )
    angle = (product % length).astype(jnp.float32) * (TWO_PI / length)
    return (jnp.cos(angle), jnp.sin(angle))


def tables():
    cosine_first, sine_first = rotation(P_SIZE, P_SIZE, P_SIZE)
    cosine_second, sine_second = rotation(Q, Q, Q)
    cosine_twist, sine_twist = rotation(Q, P_SIZE, A)
    scale_first = 1.0 / math.sqrt(P_SIZE)
    scale_second = 1.0 / math.sqrt(Q)
    return (
        (cosine_first * scale_first).astype(jnp.bfloat16),
        (sine_first * scale_first).astype(jnp.bfloat16),
        (cosine_second * scale_second).astype(jnp.bfloat16),
        (sine_second * scale_second).astype(jnp.bfloat16),
        cosine_twist,
        sine_twist,
    )


def contract(form, left, right):
    return jnp.einsum(form, left, right, preferred_element_type=jnp.float32)


def forward(planes, factors):
    cosine_first, sine_first, cosine_second, sine_second, cosine_twist, sine_twist = factors
    width = planes.shape[1]
    grid = planes.reshape(2, width, P_SIZE, Q)
    real_part = grid[0]
    imaginary = grid[1]
    first_real = contract("cpq,pf->cqf", real_part, cosine_first) + contract(
        "cpq,pf->cqf", imaginary, sine_first
    )
    first_imaginary = contract("cpq,pf->cqf", imaginary, cosine_first) - contract(
        "cpq,pf->cqf", real_part, sine_first
    )
    turned_real = (first_real * cosine_twist + first_imaginary * sine_twist).astype(jnp.bfloat16)
    turned_imaginary = (first_imaginary * cosine_twist - first_real * sine_twist).astype(
        jnp.bfloat16
    )
    second_real = contract("gq,cqf->cgf", cosine_second, turned_real) + contract(
        "gq,cqf->cgf", sine_second, turned_imaginary
    )
    second_imaginary = contract("gq,cqf->cgf", cosine_second, turned_imaginary) - contract(
        "gq,cqf->cgf", sine_second, turned_real
    )
    return jnp.stack([second_real, second_imaginary]).reshape(2, width, A).astype(jnp.bfloat16)


def inverse(planes, factors):
    cosine_first, sine_first, cosine_second, sine_second, cosine_twist, sine_twist = factors
    width = planes.shape[1]
    grid = planes.reshape(2, width, Q, P_SIZE)
    real_part = grid[0]
    imaginary = grid[1]
    first_real = contract("qg,cgf->cqf", cosine_second, real_part) - contract(
        "qg,cgf->cqf", sine_second, imaginary
    )
    first_imaginary = contract("qg,cgf->cqf", cosine_second, imaginary) + contract(
        "qg,cgf->cqf", sine_second, real_part
    )
    turned_real = (first_real * cosine_twist - first_imaginary * sine_twist).astype(jnp.bfloat16)
    turned_imaginary = (first_imaginary * cosine_twist + first_real * sine_twist).astype(
        jnp.bfloat16
    )
    second_real = contract("cqf,fp->cpq", turned_real, cosine_first) - contract(
        "cqf,fp->cpq", turned_imaginary, sine_first
    )
    second_imaginary = contract("cqf,fp->cpq", turned_imaginary, cosine_first) + contract(
        "cqf,fp->cpq", turned_real, sine_first
    )
    return jnp.stack([second_real, second_imaginary]).reshape(2, width, A).astype(jnp.bfloat16)


def body(echoes, coef_table, kern_id, band_lo, band_width, rate):
    factors = tables()
    members = lax.axis_size("az")
    here = lax.axis_index("az")
    range_rows = echoes.shape[1]
    lines = echoes.shape[2]
    columns = range_rows // members
    per_device = FBLK // members
    freq_dev = per_device * FB
    tiles = range_rows // TILE
    grouped = echoes.reshape(2, members, columns, lines)
    piece = lax.all_to_all(grouped, "az", split_axis=1, concat_axis=3, tiled=True)
    spectrum = forward(piece.reshape(2, piece.shape[2], A), factors)
    parted = spectrum.reshape(2, columns, members, freq_dev)
    turned = lax.all_to_all(parted, "az", split_axis=2, concat_axis=1, tiled=True)
    block_first = here * per_device
    block_stride = 1
    local = turned.reshape(2, range_rows, freq_dev)
    rim = HT * TILE
    padded = padded_2(local, (("rg", 1),), rim)

    def one_block(index, result):
        block = block_first + index * block_stride
        lower = band_lo[block]
        width = band_width[block]
        kernel = coef_table[kern_id[block]]
        columns_in = lax.dynamic_slice_in_dim(padded, index * FB, FB, 2)
        empty = jnp.zeros((2, tiles, TILE, FB), jnp.float32)
        total = empty
        for offset in range(WMAX):
            masked = jnp.where(offset < width, kernel[offset], jnp.zeros_like(kernel[offset]))
            start = (HT + lower + offset) * TILE
            slab = lax.dynamic_slice_in_dim(columns_in, start, range_rows, 1).reshape(
                2, tiles, TILE, FB
            )
            total = total + contract("ij,ptjf->ptif", masked, slab)
        moved = total.reshape(2, range_rows, FB)
        signed = (block * FB + lax.broadcasted_iota(jnp.int32, (FB,), 0) + A // 2) % A - A // 2
        doppler = signed.astype(jnp.float32) / A
        phase = rate[:, None] * (doppler * doppler)[None, :] * TWO_PI
        cosine = jnp.cos(phase)
        sine = jnp.sin(phase)
        focused_real = moved[0] * cosine + moved[1] * sine
        focused_imaginary = moved[1] * cosine - moved[0] * sine
        focused = jnp.stack([focused_real, focused_imaginary]).astype(jnp.bfloat16)
        return lax.dynamic_update_slice_in_dim(result, focused, index * FB, 2)

    filtered = lax.fori_loop(
        0, per_device, one_block, jnp.zeros((2, range_rows, freq_dev), jnp.bfloat16)
    )
    returned = filtered.reshape(2, members, columns, 1, freq_dev)
    piece = lax.all_to_all(returned, "az", split_axis=1, concat_axis=3, tiled=True)
    return inverse(piece.reshape(2, piece.shape[2], A), factors)


def solution(mesh):
    in_specs = (P(None, "rg", "az"), P(), P(), P(), P(), P("rg"))
    out_specs = P(None, ("rg", "az"), None)
    return jax.shard_map(body, mesh=mesh, in_specs=in_specs, out_specs=out_specs, check_vma=False)
```

profile of v0, /device:TPU:1, one launch (start us, length us, event | category | flops | bytes accessed | tf_op | source)
XLA Modules:
  0.0 264.5 jit_solution(644591594044299887)
XLA Ops:
  0.0 2.3 copy.28
  2.3 13.0 %all-to-all-start = ((bf16[2,64,8,512]{3,2,0,1:T(8,128)(2,1)}), bf16[2,64,8,512]{3,2,0,1:T(8,128)(2,1)S(1)}, u32[]{:S(2)}, u32[]{:S(2)}) async-start(bf16[2,64,8,512]{3,2,0,1:T(8,128)(2,1)} %copy.28), calls=%async_computation | async-start | bytes 2097152 | tf_op jit(solution)/shard_map/all_to_all | solution.py:120
  15.9 28.0 %all-to-all-done = bf16[2,64,8,512]{3,2,0,1:T(8,128)(2,1)S(1)} async-done(((bf16[2,64,8,512]{3,2,0,1:T(8,128)(2,1)}), bf16[2,64,8,512]{3,2,0,1:T(8,128)(2,1)S(1)}, u32[]{:S(2)}, u32[]{:S(2)}) %all-to-all-start) | async-done | bytes 1048608 | tf_op jit(solution)/shard_map/all_to_all | solution.py:120
  45.0 4.9 %fusion.71 = f32[512,512]{0,1:S(1)} fusion(bf16[512,512]{0,1:T(8,128)(2,1)S(1)} %bitcast.267), kind=kOutput, calls=%fused_computation.113 | convolution fusion | flops 272629760 | bytes 1572864
  49.9 5.7 %fusion.70 = f32[512,512]{0,1} fusion(bf16[512,512]{0,1:T(8,128)(2,1)S(1)} %bitcast.268), kind=kOutput, calls=%fused_computation.112 | convolution fusion | flops 272629760 | bytes 1572864
  56.6 4.9 %fusion.69 = f32[512,512]{0,1:S(1)} fusion(bf16[512,512]{0,1:T(8,128)(2,1)S(1)} %bitcast.269), kind=kOutput, calls=%fused_computation.111 | convolution fusion | flops 272629760 | bytes 1572864
  61.5 5.1 %fusion.72 = f32[512,512]{0,1:S(1)} fusion(bf16[512,512]{0,1:T(8,128)(2,1)S(1)} %bitcast.270), kind=kOutput, calls=%fused_computation.114 | convolution fusion | flops 272629760 | bytes 1572864
  66.6 0.6 fusion.57
  69.5 34.5 %all_to_all.45 = bf16[2,8,64,512]{3,1,0,2:T(8,128)(2,1)S(1)} all-to-all(bf16[2,8,64,512]{3,1,0,2:T(8,128)(2,1)S(1)} %copy.35), channel_id=1, replica_groups=mesh['az'=64,'rg'=4] {'az'}, dimensions={2} | all-to-all | bytes 2097152 | tf_op jit(solution)/shard_map/all_to_all | solution.py:123
  104.2 3.2 %collective-permute-start = (bf16[2,256,512]{2,1,0:T(8,128)(2,1)S(1)}, bf16[2,256,512]{2,1,0:T(8,128)(2,1)S(1)}, u32[]{:S(2)}, u32[]{:S(2)}) collective-permute-start(bf16[2,256,512]{2,1,0:T(8,128)(2,1)S(1)} %get-tuple-element.310), channel_id=1, source_target_pairs={{0,1},{1,2},{2,3},{4,5},{5,6},{6,7},{8,9},{9,10},{10,11},{12,13},{... | collective-permute-start | bytes 1572872 | tf_op jit(solution)/shard_map/ppermute | solution.py:23
  107.5 1.3 collective-permute-start.1
  108.8 9.9 %collective-permute-done = bf16[2,256,512]{2,1,0:T(8,128)(2,1)S(1)} collective-permute-done((bf16[2,256,512]{2,1,0:T(8,128)(2,1)S(1)}, bf16[2,256,512]{2,1,0:T(8,128)(2,1)S(1)}, u32[]{:S(2)}, u32[]{:S(2)}) %collective-permute-start) | collective-permute-done | bytes 524320 | tf_op jit(solution)/shard_map/ppermute | solution.py:23
  118.7 0.8 copy-done.3
  119.5 3.1 %collective-permute-done.1 = bf16[2,256,512]{2,1,0:T(8,128)(2,1)} collective-permute-done((bf16[2,256,512]{2,1,0:T(8,128)(2,1)S(1)}, bf16[2,256,512]{2,1,0:T(8,128)(2,1)}, u32[]{:S(2)}, u32[]{:S(2)}) %collective-permute-start.1) | collective-permute-done | bytes 524320 | tf_op jit(solution)/shard_map/ppermute | solution.py:26
  122.6 1.3 pad_maximum_fusion
  124.0 1.0 broadcast_in_dim.6
  125.0 75.2 %while.16 = (s32[]{:T(128)}, bf16[2,512,512]{2,1,0:T(8,128)(2,1)}, s32[]{:T(128)}, s32[256]{0:T(256)S(1)}, bf16[2,1024,512]{2,1,0:T(8,128)(2,1)S(1)}, /*index=5*...) while((s32[]{:T(128)}, bf16[2,512,512]{2,1,0:T(8,128)(2,1)}, ...), condition=%wide.region_1.2_spmd, body=%wide.region_0.1_spmd.sunk | while | flops 169560240 | bytes 11180494 | solution.py:156
  125.1 0.6 dynamic_slice.117
  128.5 2.0 constant_dynamic-slice_fusion.6
  132.8 0.6 dynamic_slice.119
  133.9 1.0 fusion.226
  135.5 1.2 convolution_add_fusion.10
  137.3 1.2 convolution_add_fusion.11
  139.0 1.2 convolution_add_fusion.12
  140.8 1.0 fusion.227
  141.9 1.3 fusion.230
  143.1 0.7 maximum_dynamic-update-slice_fusion.2
  143.9 0.6 dynamic_slice.117
  147.3 2.0 constant_dynamic-slice_fusion.6
  152.7 1.0 fusion.226
  154.3 1.2 convolution_add_fusion.10
  156.1 1.2 convolution_add_fusion.11
  157.8 1.2 convolution_add_fusion.12
  159.6 1.0 fusion.227
  160.7 1.3 fusion.230
  161.9 0.7 maximum_dynamic-update-slice_fusion.2
  162.7 0.6 dynamic_slice.117
  166.1 2.0 constant_dynamic-slice_fusion.6
  170.4 0.6 dynamic_slice.119
  171.5 1.0 fusion.226
  173.1 1.2 convolution_add_fusion.10
  174.9 1.2 convolution_add_fusion.11
  176.6 1.2 convolution_add_fusion.12
  178.4 1.0 fusion.227
  179.5 1.3 fusion.230
  180.7 0.7 maximum_dynamic-update-slice_fusion.2
  181.5 0.6 dynamic_slice.117
  184.9 2.0 constant_dynamic-slice_fusion.6
  190.3 1.0 fusion.226
  191.9 1.2 convolution_add_fusion.10
  193.7 1.2 convolution_add_fusion.11
  195.4 1.2 convolution_add_fusion.12
  197.2 1.0 fusion.227
  198.3 1.3 fusion.230
  199.5 0.7 maximum_dynamic-update-slice_fusion.2
  200.2 1.4 copy.37
  201.6 35.1 %all_to_all.46 = bf16[2,64,8,1,512]{4,2,0,3,1:T(8,128)(2,1)S(1)} all-to-all(bf16[2,64,8,1,512]{4,2,0,3,1:T(8,128)(2,1)S(1)} %copy.37), channel_id=1, replica_groups=mesh['az'=64,'rg'=4] {'az'}, dimensions={1} | all-to-all | bytes 2097152 | tf_op jit(solution)/shard_map/all_to_all | solution.py:160
  239.2 4.9 %fusion.67 = f32[512,8,64]{0,2,1:T(8,128)S(1)} fusion(bf16[8,64,512]{2,1,0:T(8,128)(2,1)S(1)} %get-tuple-element.308), kind=kOutput, calls=%fused_computation.109 | convolution fusion | flops 272629760 | bytes 1572864 | tf_op jit(solution)/shard_map/cqf,fp->cpq/dot_general | solution.py:56
  244.1 5.7 %fusion.65 = f32[512,8,64]{0,2,1:T(8,128)} fusion(bf16[8,64,512]{2,1,0:T(8,128)(2,1)S(1)} %get-tuple-element.309), kind=kOutput, calls=%fused_computation.107 | convolution fusion | flops 272629760 | bytes 1572864 | tf_op jit(solution)/shard_map/cqf,fp->cpq/dot_general | solution.py:56
  249.8 5.0 %fusion.50 = bf16[8,512,64]{1,2,0:T(8,128)(2,1)S(1)} fusion(f32[512,8,64]{0,2,1:T(8,128)S(1)} %fusion.67, bf16[8,64,512]{2,1,0:T(8,128)(2,1)S(1)} %get-tuple-element.309), kind=kOutput, calls=%fused_computation.78 | convolution fusion | flops 273154048 | bytes 2097152 | tf_op jit(solution)/shard_map/cqf,fp->cpq/dot_general | solution.py:56
  255.3 0.8 stack.39
  256.1 6.0 %fusion.49 = bf16[8,512,64]{1,2,0:T(8,128)(2,1)S(1)} fusion(f32[512,8,64]{0,2,1:T(8,128)} %fusion.65, bf16[8,64,512]{2,1,0:T(8,128)(2,1)S(1)} %get-tuple-element.308), kind=kOutput, calls=%fused_computation.77 | convolution fusion | flops 273154048 | bytes 2097152 | tf_op jit(solution)/shard_map/cqf,fp->cpq/dot_general | solution.py:56
  262.6 0.8 stack.40
  263.4 1.1 pad_maximum_fusion.2
  (52 shorter events, 12.1 us)
Async XLA Ops:
  2.3 41.5 %all-to-all-start = ((bf16[2,64,8,512]{3,2,0,1:T(8,128)(2,1)}), bf16[2,64,8,512]{3,2,0,1:T(8,128)(2,1)S(1)}, u32[]{:S(2)}, u32[]{:S(2)}) async-start(bf16[2,64,8,512]{3,2,0,1:T(8,128)(2,1)} %copy.28), calls=%async_computation | async-start | bytes 2097152 | tf_op jit(solution)/shard_map/all_to_all | solution.py:120
  15.9 50.7 %copy-start = (f32[64,512]{1,0:T(8,128)}, f32[64,512]{1,0:T(8,128)S(1)}, u32[]{:S(2)}) copy-start(f32[64,512]{1,0:T(8,128)S(1)} %get-tuple-element.315) | copy-start | bytes 393220
  61.5 5.1 %copy-start.2 = (f32[512,512]{0,1:S(1)}, f32[512,512]{0,1}, u32[]{:S(2)}) copy-start(f32[512,512]{0,1} %fusion.70) | copy-start | bytes 3145732
  104.2 14.5 %collective-permute-start = (bf16[2,256,512]{2,1,0:T(8,128)(2,1)S(1)}, bf16[2,256,512]{2,1,0:T(8,128)(2,1)S(1)}, u32[]{:S(2)}, u32[]{:S(2)}) collective-permute-start(bf16[2,256,512]{2,1,0:T(8,128)(2,1)S(1)} %get-tuple-element.310), channel_id=1, source_target_pairs={{0,1},{1,2},{2,3},{4,5},{5,6},{6,7},{8,9},{9,10},{10,11},{12,13},{... | collective-permute-start | bytes 1572872 | tf_op jit(solution)/shard_map/ppermute | solution.py:23
  107.5 15.2 %collective-permute-start.1 = (bf16[2,256,512]{2,1,0:T(8,128)(2,1)S(1)}, bf16[2,256,512]{2,1,0:T(8,128)(2,1)}, u32[]{:S(2)}, u32[]{:S(2)}) collective-permute-start(bf16[2,256,512]{2,1,0:T(8,128)(2,1)S(1)} %get-tuple-element.311), channel_id=1, source_target_pairs={{1,0},{2,1},{3,2},{5,4},{6,5},{7,6},{9,8},{10,9},{11,10},{13,12},{... | collective-permute-start | bytes 1572872 | tf_op jit(solution)/shard_map/ppermute | solution.py:26
  108.8 16.2 %copy-start.4 = (f32[512]{0:T(512)S(1)}, f32[512]{0:T(512)}, u32[]{:S(2)}) copy-start(f32[512]{0:T(512)} %param.13) | copy-start | bytes 6148
  108.8 16.2 %copy-start.5 = (s32[256]{0:T(256)S(1)}, s32[256]{0:T(256)}, u32[]{:S(2)}) copy-start(s32[256]{0:T(256)} %param.11) | copy-start | bytes 3076
  108.8 16.2 %copy-start.6 = (s32[256]{0:T(256)S(1)}, s32[256]{0:T(256)}, u32[]{:S(2)}) copy-start(s32[256]{0:T(256)} %param.12) | copy-start | bytes 3076
  108.8 16.2 %copy-start.7 = (s32[256]{0:T(256)S(1)}, s32[256]{0:T(256)}, u32[]{:S(2)}) copy-start(s32[256]{0:T(256)} %param.10) | copy-start | bytes 3076
  118.7 0.8 copy-start.3
  237.7 0.9 copy-start.1
where the time goes:
time: 266 us; the launch traced here: 264 us
  blocking collectives  69.7 us (26%)
  matrix products  67.5 us (25%)
  waiting for transfers between devices  41 us (15%)
  loops' own time  29.9 us (11%)
  local copies, waits for them, and re-layouts  26.9 us (10%)
  starting transfers between devices  17.5 us (7%)
  other arithmetic  11.6 us (4%)
    dot_general x32, matrix products, contract(): return jnp.einsum(form, left, right, preferred_element_type=jnp.float32)  47 us
    all_to_all x1, blocking collectives, body(): lax.all_to_all(returned, 'az', split_axis=1, concat_axis=3, tiled=True)  35.1 us
    all_to_all x1, blocking collectives, body(): lax.all_to_all(parted, 'az', split_axis=2, concat_axis=1, tiled=True)  34.5 us
    another operation x1, loops' own time, body(): lax.fori_loop(0, per_device, one_block, jnp.zeros((2, range_rows, freq_de...  29.9 us
    all_to_all x1, waiting for transfers between devices, body(): lax.all_to_all(grouped, 'az', split_axis=1, concat_axis=3, tiled=True)  28 us
    unnamed x4, matrix products  20.5 us
    all_to_all x1, starting transfers between devices, body(): lax.all_to_all(grouped, 'az', split_axis=1, concat_axis=3, tiled=True)  13 us
    ppermute x1, waiting for transfers between devices, padded_2(): lax.ppermute(lax.slice_in_dim(block, block.shape[dim] - width, None, axis...  9.87 us
  transfers between devices with their start and end apart: 3, of which 3 were waited for; matrix products, arithmetic and copies ran while one was open for 0% of the time, Pallas kernels for 0%

commit v1 on v0

--- a/solution.py
+++ b/solution.py
@@ -120,7 +120,10 @@
     piece = lax.all_to_all(grouped, "az", split_axis=1, concat_axis=3, tiled=True)
     spectrum = forward(piece.reshape(2, piece.shape[2], A), factors)
     parted = spectrum.reshape(2, columns, members, freq_dev)
-    turned = lax.all_to_all(parted, "az", split_axis=2, concat_axis=1, tiled=True)
+    peers = lax.axis_size("az")
+    tiles_2 = jnp.stack(jnp.split(parted, peers, axis=2), axis=0)
+    tiles_2 = lax.all_to_all(tiles_2, "az", split_axis=0, concat_axis=0)
+    turned = jnp.concatenate(tiles_2, axis=1)
     block_first = here * per_device
     block_stride = 1
     local = turned.reshape(2, range_rows, freq_dev)

time: 266 us -> 275 us (1.034)
  loops' own time: 29.9 us -> 34.3 us
    another operation x1, loops' own time: 29.9 us -> 34.3 us  [body(): lax.fori_loop(0, per_device, one_block, jnp.zeros((2, range_rows, freq_de...]
where the time goes in v1:
time: 275 us; the launch traced here: 273 us
  blocking collectives  69.7 us (25%)
  matrix products  67.5 us (25%)
  waiting for transfers between devices  41 us (15%)
  loops' own time  34.3 us (12%)
  local copies, waits for them, and re-layouts  27.8 us (10%)
  starting transfers between devices  17.5 us (6%)
  other arithmetic  14.3 us (5%)
    dot_general x32, matrix products, contract(): return jnp.einsum(form, left, right, preferred_element_type=jnp.float32)  47 us
    all_to_all x1, blocking collectives, body(): lax.all_to_all(returned, 'az', split_axis=1, concat_axis=3, tiled=True)  35.2 us
    all_to_all x1, blocking collectives, body(): tiles_2 = lax.all_to_all(tiles_2, 'az', split_axis=0, concat_axis=0)  34.5 us
    another operation x1, loops' own time, body(): lax.fori_loop(0, per_device, one_block, jnp.zeros((2, range_rows, freq_de...  34.3 us
    all_to_all x1, waiting for transfers between devices, body(): lax.all_to_all(grouped, 'az', split_axis=1, concat_axis=3, tiled=True)  28 us
    unnamed x4, matrix products  20.5 us
    all_to_all x1, starting transfers between devices, body(): lax.all_to_all(grouped, 'az', split_axis=1, concat_axis=3, tiled=True)  13 us
    ppermute x1, waiting for transfers between devices, padded_2(): lax.ppermute(lax.slice_in_dim(block, block.shape[dim] - width, None, axis...  9.87 us
  transfers between devices with their start and end apart: 3, of which 3 were waited for; matrix products, arithmetic and copies ran while one was open for 0% of the time, Pallas kernels for 0%

profile of v1, /device:TPU:1, one launch (start us, length us, event | category | flops | bytes accessed | tf_op | source)
XLA Modules:
  0.0 273.0 jit_solution(8737664255932335197)
XLA Ops:
  0.0 2.3 copy.1774
  2.3 13.0 %all-to-all-start = ((bf16[2,64,8,512]{3,2,0,1:T(8,128)(2,1)}), bf16[2,64,8,512]{3,2,0,1:T(8,128)(2,1)S(1)}, u32[]{:S(2)}, u32[]{:S(2)}) async-start(bf16[2,64,8,512]{3,2,0,1:T(8,128)(2,1)} %copy.1774), calls=%async_computation | async-start | bytes 2097152 | tf_op jit(solution)/shard_map/all_to_all | solution.py:120
  15.9 28.0 %all-to-all-done = bf16[2,64,8,512]{3,2,0,1:T(8,128)(2,1)S(1)} async-done(((bf16[2,64,8,512]{3,2,0,1:T(8,128)(2,1)}), bf16[2,64,8,512]{3,2,0,1:T(8,128)(2,1)S(1)}, u32[]{:S(2)}, u32[]{:S(2)}) %all-to-all-start) | async-done | bytes 1048608 | tf_op jit(solution)/shard_map/all_to_all | solution.py:120
  45.5 4.9 %fusion.71 = f32[512,512]{0,1:S(1)} fusion(bf16[512,512]{0,1:T(8,128)(2,1)S(1)} %bitcast.393), kind=kOutput, calls=%fused_computation.239 | convolution fusion | flops 272629760 | bytes 1572864
  50.4 5.7 %fusion.70 = f32[512,512]{0,1} fusion(bf16[512,512]{0,1:T(8,128)(2,1)S(1)} %bitcast.394), kind=kOutput, calls=%fused_computation.238 | convolution fusion | flops 272629760 | bytes 1572864
  56.9 4.9 %fusion.69 = f32[512,512]{0,1:S(1)} fusion(bf16[512,512]{0,1:T(8,128)(2,1)S(1)} %bitcast.395), kind=kOutput, calls=%fused_computation.237 | convolution fusion | flops 272629760 | bytes 1572864
  61.8 5.1 %fusion.72 = f32[512,512]{0,1:S(1)} fusion(bf16[512,512]{0,1:T(8,128)(2,1)S(1)} %bitcast.396), kind=kOutput, calls=%fused_computation.240 | convolution fusion | flops 272629760 | bytes 1572864
  72.8 34.5 %all_to_all.35 = bf16[64,2,8,1,512]{4,2,1,3,0:T(8,128)(2,1)S(1)} all-to-all(bf16[64,2,8,1,512]{4,2,1,3,0:T(8,128)(2,1)S(1)} %constant_dynamic-update-slice_fusion), channel_id=1, replica_groups=mesh['az'=64,'rg'=4] {'az'}, dimensions={0} | all-to-all | bytes 2097152 | tf_op jit(solution)/shard_map/all_to_all | solution.py:125
  107.5 3.2 %collective-permute-start = (bf16[2,256,512]{2,1,0:T(8,128)(2,1)S(1)}, bf16[2,256,512]{2,1,0:T(8,128)(2,1)S(1)}, u32[]{:S(2)}, u32[]{:S(2)}) collective-permute-start(bf16[2,256,512]{2,1,0:T(8,128)(2,1)S(1)} %get-tuple-element.310), channel_id=1, source_target_pairs={{0,1},{1,2},{2,3},{4,5},{5,6},{6,7},{8,9},{9,10},{10,11},{12,13},{... | collective-permute-start | bytes 1572872 | tf_op jit(solution)/shard_map/ppermute | solution.py:23
  110.8 1.3 collective-permute-start.1
  112.1 9.9 %collective-permute-done = bf16[2,256,512]{2,1,0:T(8,128)(2,1)S(1)} collective-permute-done((bf16[2,256,512]{2,1,0:T(8,128)(2,1)S(1)}, bf16[2,256,512]{2,1,0:T(8,128)(2,1)S(1)}, u32[]{:S(2)}, u32[]{:S(2)}) %collective-permute-start) | collective-permute-done | bytes 524320 | tf_op jit(solution)/shard_map/ppermute | solution.py:23
  122.0 0.8 copy-done.3
  122.8 3.1 %collective-permute-done.1 = bf16[2,256,512]{2,1,0:T(8,128)(2,1)} collective-permute-done((bf16[2,256,512]{2,1,0:T(8,128)(2,1)S(1)}, bf16[2,256,512]{2,1,0:T(8,128)(2,1)}, u32[]{:S(2)}, u32[]{:S(2)}) %collective-permute-start.1) | collective-permute-done | bytes 524320 | tf_op jit(solution)/shard_map/ppermute | solution.py:26
  125.9 1.3 pad_maximum_fusion
  127.3 1.0 broadcast_in_dim.6
  128.3 80.4 %while.16 = (s32[]{:T(128)}, bf16[2,512,512]{2,1,0:T(8,128)(2,1)}, s32[]{:T(128)}, s32[256]{0:T(256)S(1)}, bf16[2,1024,512]{2,1,0:T(8,128)(2,1)S(1)}, /*index=5*...) while((s32[]{:T(128)}, bf16[2,512,512]{2,1,0:T(8,128)(2,1)}, ...), condition=%wide.region_1.2_spmd, body=%wide.region_0.1_spmd.sunk | while | flops 169560240 | bytes 11180494 | solution.py:159
  128.4 0.7 dynamic_slice.117
  132.4 2.0 constant_dynamic-slice_fusion.6
  134.4 0.6 dynamic_slice.118
  137.0 0.7 dynamic_slice.119
  138.3 1.0 fusion.290
  139.9 1.2 convolution_add_fusion.10
  141.7 1.2 convolution_add_fusion.11
  143.6 1.2 convolution_add_fusion.12
  145.4 1.0 fusion.291
  146.5 1.3 fusion.294
  147.7 0.7 maximum_dynamic-update-slice_fusion.2
  152.5 2.0 constant_dynamic-slice_fusion.6
  157.1 0.7 dynamic_slice.119
  158.4 1.0 fusion.290
  160.0 1.2 convolution_add_fusion.10
  161.8 1.2 convolution_add_fusion.11
  163.7 1.2 convolution_add_fusion.12
  165.5 1.0 fusion.291
  166.6 1.3 fusion.294
  167.8 0.7 maximum_dynamic-update-slice_fusion.2
  172.6 2.0 constant_dynamic-slice_fusion.6
  177.2 0.7 dynamic_slice.119
  178.5 1.0 fusion.290
  180.1 1.2 convolution_add_fusion.10
  181.9 1.2 convolution_add_fusion.11
  183.8 1.2 convolution_add_fusion.12
  185.6 1.0 fusion.291
  186.7 1.3 fusion.294
  187.9 0.7 maximum_dynamic-update-slice_fusion.2
  192.7 2.0 constant_dynamic-slice_fusion.6
  194.7 0.6 dynamic_slice.118
  197.3 0.7 dynamic_slice.119
  198.6 1.0 fusion.290
  200.2 1.2 convolution_add_fusion.10
  202.0 1.2 convolution_add_fusion.11
  203.9 1.2 convolution_add_fusion.12
  205.7 1.0 fusion.291
  206.8 1.3 fusion.294
  208.0 0.7 maximum_dynamic-update-slice_fusion.2
  208.8 1.4 copy.1781
  210.1 35.2 %all_to_all.36 = bf16[2,64,8,1,512]{4,2,0,3,1:T(8,128)(2,1)S(1)} all-to-all(bf16[2,64,8,1,512]{4,2,0,3,1:T(8,128)(2,1)S(1)} %copy.1781), channel_id=1, replica_groups=mesh['az'=64,'rg'=4] {'az'}, dimensions={1} | all-to-all | bytes 2097152 | tf_op jit(solution)/shard_map/all_to_all | solution.py:163
  247.7 4.9 %fusion.67 = f32[512,8,64]{0,2,1:T(8,128)S(1)} fusion(bf16[8,64,512]{2,1,0:T(8,128)(2,1)S(1)} %get-tuple-element.308), kind=kOutput, calls=%fused_computation.235 | convolution fusion | flops 272629760 | bytes 1572864 | tf_op jit(solution)/shard_map/cqf,fp->cpq/dot_general | solution.py:56
  252.6 5.7 %fusion.65 = f32[512,8,64]{0,2,1:T(8,128)} fusion(bf16[8,64,512]{2,1,0:T(8,128)(2,1)S(1)} %get-tuple-element.309), kind=kOutput, calls=%fused_computation.233 | convolution fusion | flops 272629760 | bytes 1572864 | tf_op jit(solution)/shard_map/cqf,fp->cpq/dot_general | solution.py:56
  258.3 5.0 %fusion.50 = bf16[8,512,64]{1,2,0:T(8,128)(2,1)S(1)} fusion(f32[512,8,64]{0,2,1:T(8,128)S(1)} %fusion.67, bf16[8,64,512]{2,1,0:T(8,128)(2,1)S(1)} %get-tuple-element.309), kind=kOutput, calls=%fused_computation.204 | convolution fusion | flops 273154048 | bytes 2097152 | tf_op jit(solution)/shard_map/cqf,fp->cpq/dot_general | solution.py:56
  263.8 0.8 stack.299
  264.6 6.0 %fusion.49 = bf16[8,512,64]{1,2,0:T(8,128)(2,1)S(1)} fusion(f32[512,8,64]{0,2,1:T(8,128)} %fusion.65, bf16[8,64,512]{2,1,0:T(8,128)(2,1)S(1)} %get-tuple-element.308), kind=kOutput, calls=%fused_computation.203 | convolution fusion | flops 273154048 | bytes 2097152 | tf_op jit(solution)/shard_map/cqf,fp->cpq/dot_general | solution.py:56
  271.1 0.8 stack.300
  271.9 1.1 pad_maximum_fusion.1
  (121 shorter events, 15.3 us)
Async XLA Ops:
  2.3 41.5 %all-to-all-start = ((bf16[2,64,8,512]{3,2,0,1:T(8,128)(2,1)}), bf16[2,64,8,512]{3,2,0,1:T(8,128)(2,1)S(1)}, u32[]{:S(2)}, u32[]{:S(2)}) async-start(bf16[2,64,8,512]{3,2,0,1:T(8,128)(2,1)} %copy.1774), calls=%async_computation | async-start | bytes 2097152 | tf_op jit(solution)/shard_map/all_to_all | solution.py:120
  15.9 51.0 %copy-start = (f32[64,512]{1,0:T(8,128)}, f32[64,512]{1,0:T(8,128)S(1)}, u32[]{:S(2)}) copy-start(f32[64,512]{1,0:T(8,128)S(1)} %get-tuple-element.378) | copy-start | bytes 393220
  61.8 5.1 %copy-start.2 = (f32[512,512]{0,1:S(1)}, f32[512,512]{0,1}, u32[]{:S(2)}) copy-start(f32[512,512]{0,1} %fusion.70) | copy-start | bytes 3145732
  107.5 14.5 %collective-permute-start = (bf16[2,256,512]{2,1,0:T(8,128)(2,1)S(1)}, bf16[2,256,512]{2,1,0:T(8,128)(2,1)S(1)}, u32[]{:S(2)}, u32[]{:S(2)}) collective-permute-start(bf16[2,256,512]{2,1,0:T(8,128)(2,1)S(1)} %get-tuple-element.310), channel_id=1, source_target_pairs={{0,1},{1,2},{2,3},{4,5},{5,6},{6,7},{8,9},{9,10},{10,11},{12,13},{... | collective-permute-start | bytes 1572872 | tf_op jit(solution)/shard_map/ppermute | solution.py:23
  110.8 15.2 %collective-permute-start.1 = (bf16[2,256,512]{2,1,0:T(8,128)(2,1)S(1)}, bf16[2,256,512]{2,1,0:T(8,128)(2,1)}, u32[]{:S(2)}, u32[]{:S(2)}) collective-permute-start(bf16[2,256,512]{2,1,0:T(8,128)(2,1)S(1)} %get-tuple-element.311), channel_id=1, source_target_pairs={{1,0},{2,1},{3,2},{5,4},{6,5},{7,6},{9,8},{10,9},{11,10},{13,12},{... | collective-permute-start | bytes 1572872 | tf_op jit(solution)/shard_map/ppermute | solution.py:26
  112.1 16.2 %copy-start.4 = (f32[512]{0:T(512)S(1)}, f32[512]{0:T(512)}, u32[]{:S(2)}) copy-start(f32[512]{0:T(512)} %param.13) | copy-start | bytes 6148
  112.1 16.2 %copy-start.5 = (s32[256]{0:T(256)S(1)}, s32[256]{0:T(256)}, u32[]{:S(2)}) copy-start(s32[256]{0:T(256)} %param.11) | copy-start | bytes 3076
  112.1 16.2 %copy-start.6 = (s32[256]{0:T(256)S(1)}, s32[256]{0:T(256)}, u32[]{:S(2)}) copy-start(s32[256]{0:T(256)} %param.12) | copy-start | bytes 3076
  112.1 16.2 %copy-start.7 = (s32[256]{0:T(256)S(1)}, s32[256]{0:T(256)}, u32[]{:S(2)}) copy-start(s32[256]{0:T(256)} %param.10) | copy-start | bytes 3076
  122.0 0.8 copy-start.3
  246.2 0.9 copy-start.1
